TPU v7x, 32 devices: a whole 2x2x4 slice. The times are simulated.
32 devices in a mesh: groups: 2 (over y), seq: 4 (over z), dp: 4 (over x, core).
Axes of the slice: x: 2, y: 2, z: 4, core: 2. Of those that a mesh axis runs over, the one named last changes fastest.
Arguments:
- inputs: bfloat16 [8, 4096, 448], P(('groups', 'dp'), 'seq'), parts along dimension 0, may hold values from -6 to 6
- cotangent: bfloat16 [8, 4096, 448], P(('groups', 'dp'), 'seq'), parts along dimension 0, may hold values from -6 to 6
- first_weight_matrix: bfloat16 [3, 448, 448], P(None, None, 'dp'), may hold values from -0.15625 to 0.15625
- weight_two: bfloat16 [3, 448, 448], P(None, None, 'dp'), may hold values from -0.15625 to 0.15625
Outputs:
- input_grad: bfloat16 [8, 4096, 448], P(('groups', 'dp'), 'seq'), parts along dimension 0
- grad_one: float32 [6, 448, 448], P('groups', None, 'dp'), parts along dimension 0
- grad_two: float32 [6, 448, 448], P('groups', None, 'dp'), parts along dimension 0
There are 2 independent parts, one for each index of `groups`. A program takes and returns all parts, laid end to end along the dimension named above; an argument that names none is the same for every part. Nothing has to cross between parts.
All inputs are finite; a program needn't handle non-finite values.
Results may differ from a plain program's by a relative error of at most 0.012.
Values may be sent and summed in bfloat16 or wider, within the bound.
No kernel may reach another device: no remote copies, remote signals or barrier semaphores. Data moves between devices by JAX's collectives and lax.ppermute only.
A program may use at most 64 MiB of HBM per device.

v0:
```python
import math
import jax
import jax.numpy as jnp
from jax import lax
from jax.sharding import PartitionSpec as P


def shifted(block, axis, distance):
    devices = range(lax.axis_size(axis))
    route = [(i - distance, i) for i in devices if i - distance in devices]
    return lax.ppermute(block, axis, route)


def gelu_slope(value):
    return jax.vjp(jax.nn.gelu, value)[1](jnp.ones_like(value))[0]


def outer_terms(left, right, factor):
    product = lax.dot_general(
        left, right, (((0,), (0,)), ((), ())), preferred_element_type=jnp.float32
    )
    return product * factor


def back_product(tap, weight):
    return lax.dot_general(
        tap, weight, (((1,), (1,)), ((), ())), preferred_element_type=jnp.float32
    )


def on_device(inputs, cotangent, first_weight_matrix, weight_two):
    chans = inputs.shape[2]
    rows = inputs.shape[0] * inputs.shape[1]
    factor = 1.0 / math.sqrt(
        inputs.shape[0] * lax.axis_size("dp") * inputs.shape[1] * lax.axis_size("seq")
    )
    full_one = lax.all_gather(first_weight_matrix, "dp", axis=2, tiled=True)
    flat_in = inputs.reshape(rows, chans)
    inputs_f = flat_in.astype(jnp.float32)
    input_activation = jax.nn.gelu(inputs_f).astype(jnp.bfloat16)
    act_before = shifted(input_activation, "seq", 2)
    act_after = shifted(input_activation, "seq", -2)
    flat_cot = cotangent.reshape(rows, chans)
    cot_later = shifted(flat_cot, "seq", -4)
    cot_earlier = shifted(flat_cot, "seq", 4)
    preactivation = jnp.dot(act_before, full_one[0], preferred_element_type=jnp.float32)
    preactivation = preactivation + jnp.dot(
        input_activation, full_one[1], preferred_element_type=jnp.float32
    )
    preactivation = preactivation + jnp.dot(
        act_after, full_one[2], preferred_element_type=jnp.float32
    )
    hidden_f = (inputs_f + preactivation).astype(jnp.bfloat16).astype(jnp.float32)
    act_one = jax.nn.gelu(hidden_f).astype(jnp.bfloat16)
    full_two = lax.all_gather(weight_two, "dp", axis=2, tiled=True)
    second_layer_taps = (cot_later, flat_cot, cot_earlier)
    delta_one = back_product(second_layer_taps[0], full_two[0])
    delta_one = delta_one + back_product(second_layer_taps[1], full_two[1])
    delta_one = delta_one + back_product(second_layer_taps[2], full_two[2])
    middle_gradient = (flat_cot.astype(jnp.float32) + gelu_slope(hidden_f) * delta_one).astype(
        jnp.bfloat16
    )
    part_two = jnp.stack(
        [outer_terms(act_one, second_layer_taps[k], factor) for k in range(3)]
    ).astype(jnp.bfloat16)
    grad_two = lax.psum(
        lax.psum_scatter(part_two, "dp", scatter_dimension=2, tiled=True).astype(jnp.float32), "seq"
    )
    grad_later = shifted(middle_gradient, "seq", -2)
    grad_earlier = shifted(middle_gradient, "seq", 2)
    first_layer_taps = (grad_later, middle_gradient, grad_earlier)
    delta_zero = back_product(first_layer_taps[0], full_one[0])
    delta_zero = delta_zero + back_product(first_layer_taps[1], full_one[1])
    delta_zero = delta_zero + back_product(first_layer_taps[2], full_one[2])
    input_grad = (middle_gradient.astype(jnp.float32) + gelu_slope(inputs_f) * delta_zero).astype(
        jnp.bfloat16
    )
    part_one = jnp.stack(
        [outer_terms(input_activation, first_layer_taps[k], factor) for k in range(3)]
    ).astype(jnp.bfloat16)
    grad_one = lax.psum(
        lax.psum_scatter(part_one, "dp", scatter_dimension=2, tiled=True).astype(jnp.float32), "seq"
    )
    return (input_grad.reshape(inputs.shape), grad_one, grad_two)


def solution(mesh):
    placed = (
        P(("groups", "dp"), "seq", None),
        P(("groups", "dp"), "seq", None),
        P(None, None, "dp"),
        P(None, None, "dp"),
    )
    return jax.shard_map(
        on_device,
        mesh=mesh,
        in_specs=placed,
        out_specs=(
            P(("groups", "dp"), "seq", None),
            P("groups", None, "dp"),
            P("groups", None, "dp"),
        ),
        check_vma=False,
    )
```

profile of v0, /device:TPU:0, one launch (start us, length us, event | category | flops | bytes accessed | tf_op | source)
XLA Modules:
  0.0 242.5 jit_solution(234301999639612765)
XLA Ops:
  7.2 0.0 copy-start.2
  7.2 0.0 all-gather.3.cloned.1.call-start
  7.2 2.2 copy.9
  9.4 0.0 all-gather.3.cloned.1.call-update
  9.4 0.0 all-gather.5.cloned.1.call-start
  9.5 2.1 copy.13
  11.6 0.0 all-gather.5.cloned.1.call-update
  11.6 0.0 reduce-scatter.9.cloned.1.call-start
  11.7 1.6 fusion.26
  13.2 6.9 %collective-permute-start = (bf16[1024,448]{0,1:T(8,128)(2,1)}, bf16[1024,448]{0,1:T(8,128)(2,1)}, u32[]{:S(2)}, u32[]{:S(2)}) collective-permute-start(bf16[1024,448]{0,1:T(8,128)(2,1)} %fusion.26), channel_id=1, source_target_pairs={{0,8},{4,12},{1,9},{5,13},{2,10},{6,14},{3,11},{7,15},{16,24},{20,... | collective-permute-start | bytes 2752520 | tf_op jit(solution)/shard_map/ppermute | solution.py:11
  20.1 1.3 collective-permute-start.1
  21.4 1.6 collective-permute-start.2
  23.0 11.0 %all-gather.3.cloned.1.call-done = bf16[3,448,448]{1,0,2:T(4,128)(2,1)} async-done(((bf16[3,448,112]{1,0,2:T(4,128)(2,1)}), bf16[3,448,448]{1,0,2:T(4,128)(2,1)}) %all-gather.3.cloned.1.call-update) | async-done | bytes 1204240 | tf_op jit(solution)/shard_map/all_gather | solution.py:37
  34.0 6.1 %fusion.88 = (bf16[1,448,448]{1,0,2:T(2,128)(2,1)S(1)}, bf16[1,448,448]{1,0,2:T(2,128)(2,1)S(1)}, bf16[1,448,448]{1,0,2:T(2,128)(2,1)}) fusion(bf16[3,448,448]{1,0,2:T(4,128)(2,1)} %all-gather.3.cloned.1.call-done), kind=kLoop, calls=%fused_computation.93 | loop fusion | bytes 2408448 | tf_op jit(solution)/shard_map/slice | solution.py:51
  40.1 17.2 %all-gather.5.cloned.1.call-done = bf16[3,448,448]{1,0,2:T(4,128)(2,1)} async-done(((bf16[3,448,112]{1,0,2:T(4,128)(2,1)}), bf16[3,448,448]{1,0,2:T(4,128)(2,1)}) %all-gather.5.cloned.1.call-update) | async-done | bytes 1204240 | tf_op jit(solution)/shard_map/all_gather | solution.py:55
  57.3 6.3 %fusion.87 = (bf16[1,448,448]{1,0,2:T(2,128)(2,1)}, bf16[1,448,448]{1,0,2:T(2,128)(2,1)}, bf16[1,448,448]{1,0,2:T(2,128)(2,1)}) fusion(bf16[3,448,448]{1,0,2:T(4,128)(2,1)} %all-gather.5.cloned.1.call-done), kind=kLoop, calls=%fused_computation.92 | loop fusion | bytes 2408448 | tf_op jit(solution)/shard_map/slice | solution.py:59
  63.6 2.4 copy.21
  66.0 2.0 copy.22
  68.0 1.9 copy.23
  69.9 3.5 %copy.24 = bf16[1,448,448]{2,1,0:T(8,128)(2,1)} copy(bf16[1,448,448]{1,0,2:T(2,128)(2,1)} %get-tuple-element.7) | data formatting | bytes 802816
  73.4 1.3 copy.25
  74.7 1.0 fusion.46
  75.7 3.1 %fusion.57 = f32[1024,448]{0,1:T(8,128)} fusion(bf16[1,448,448]{2,1,0:T(8,128)(2,1)S(1)} %copy.25, bf16[1,1024,448]{1,2,0:T(8,128)(2,1)} %param.5), kind=kOutput, calls=%fused_computation.71 | convolution fusion | flops 411041792 | bytes 3153920 | tf_op jit(solution)/shard_map/dot_general | solution.py:26
  78.8 1.9 fusion.74
  80.8 2.1 fusion.27
  82.8 0.0 copy-start.17
  82.8 2.3 fusion.40
  85.2 2.0 fusion.41
  87.2 0.2 pad_maximum_fusion.1
  87.4 1.8 copy.19
  89.2 2.5 %reshape.22 = bf16[448,1344]{1,0:T(8,128)(2,1)} reshape(bf16[448,3,448]{2,1,0:T(4,128)(2,1)S(1)} %bitcast.119) | data formatting | bytes 2408448
  91.7 0.0 reduce-scatter.9.cloned.1.call-update
  91.8 0.2 reduce-scatter.7.cloned.1.call-start
  92.0 3.2 %fusion.59 = f32[1024,448]{0,1:T(8,128)} fusion(bf16[1024,448]{0,1:T(8,128)(2,1)} %collective-permute-done.2, bf16[1,448,448]{2,1,0:T(8,128)(2,1)S(1)} %copy-done.10), kind=kOutput, calls=%fused_computation.73 | convolution fusion | flops 411041792 | bytes 3153920 | tf_op jit(solution)/shard_map/dot_general | solution.py:26
  95.2 1.3 copy.26
  96.5 0.0 copy-start.3
  96.5 4.2 %fusion.17 = bf16[1024,448]{0,1:T(8,128)(2,1)S(1)} fusion(bf16[1024,448]{0,1:T(8,128)(2,1)} %copy-done.17, f32[1024,448]{0,1:T(8,128)} %fusion.59, f32[1024,448]{0,1:T(8,128)S(1)} %copy-done.7, bf16[1024,448]{0,1:T(8,128)(2,1)} %collective-permute-done.2, bf16[1,448,448]{2,1,0:T(8,128)(2,1)S(1)} %copy.26, bf16[1,1024,448]{1,2,0:T(8,128)(2,1)} %param.5), kind=kOutput, calls=%fused_computation.27 | convolution fusion | flops 422051840 | bytes 7741440 | tf_op jit(solution)/shard_map/dot_general | solution.py:26
  100.7 4.5 %collective-permute-start.4 = (bf16[1024,448]{0,1:T(8,128)(2,1)S(1)}, bf16[1024,448]{0,1:T(8,128)(2,1)S(1)}, u32[]{:S(2)}, u32[]{:S(2)}) collective-permute-start(bf16[1024,448]{0,1:T(8,128)(2,1)S(1)} %fusion.17), channel_id=1, source_target_pairs={{0,8},{4,12},{1,9},{5,13},{2,10},{6,14},{3,11},{7,15},{16,24},{20,... | collective-permute-start | bytes 2752520 | tf_op jit(solution)/shard_map/ppermute | solution.py:11
  105.2 1.3 collective-permute-start.3
  106.5 0.8 fusion.43
  107.4 17.8 %collective-permute-done.4 = bf16[1024,448]{0,1:T(8,128)(2,1)S(1)} collective-permute-done((bf16[1024,448]{0,1:T(8,128)(2,1)S(1)}, bf16[1024,448]{0,1:T(8,128)(2,1)S(1)}, u32[]{:S(2)}, u32[]{:S(2)}) %collective-permute-start.4) | collective-permute-done | bytes 917536 | tf_op jit(solution)/shard_map/ppermute | solution.py:11
  125.2 0.8 fusion.42
  126.0 0.1 copy-done.18
  126.1 23.8 %collective-permute-done.3 = bf16[1024,448]{0,1:T(8,128)(2,1)S(1)} collective-permute-done((bf16[1024,448]{0,1:T(8,128)(2,1)S(1)}, bf16[1024,448]{0,1:T(8,128)(2,1)S(1)}, u32[]{:S(2)}, u32[]{:S(2)}) %collective-permute-start.3) | collective-permute-done | bytes 917536 | tf_op jit(solution)/shard_map/ppermute | solution.py:11
  149.9 0.9 copy-done.15
  150.8 0.8 fusion.44
  151.6 0.2 pad_maximum_fusion
  151.8 1.8 copy.17
  153.6 2.5 %reshape.20 = bf16[448,1344]{1,0:T(8,128)(2,1)} reshape(bf16[448,3,448]{2,1,0:T(4,128)(2,1)S(1)} %bitcast.120) | data formatting | bytes 2408448
  156.1 0.0 reduce-scatter.7.cloned.1.call-update
  156.2 0.6 fusion.69
  156.9 0.4 copy-done.1
  157.2 0.3 copy-done.16
  157.5 0.6 fusion.72
  158.2 0.5 copy-done.4
  158.7 0.1 copy-done.12
  158.8 0.5 copy-done.19
  159.3 2.7 %fusion.52 = bf16[1,1024,448]{1,2,0:T(8,128)(2,1)} fusion(f32[1024,448]{0,1:T(8,128)S(1)} %fusion.72, f32[1024,448]{0,1:T(8,128)S(1)} %fusion.69, bf16[1,1024,448]{1,2,0:T(8,128)(2,1)S(1)} %copy-done.4, bf16[1024,448]{0,1:T(8,128)(2,1)S(1)} %copy-done.14, bf16[1024,448]{0,1:T(8,128)(2,1)S(1)} %copy-done.19, bf16[1,448,448]{2,1,0:T(8,128)(2,1)S(1)} %copy-done.12), kind=kOutput, calls=%fused_computation.68 | convolution fusion | flops 422051840 | bytes 7741440 | tf_op jit(solution)/shard_map/dot_general | solution.py:26
  162.0 1.7 reshape.23
  163.7 0.3 copy.20
  164.0 15.7 %reduce-scatter.7.cloned.1.call-done = bf16[112,1344]{1,0:T(8,128)(2,1)} async-done(((bf16[448,1344]{1,0:T(8,128)(2,1)}), bf16[112,1344]{1,0:T(8,128)(2,1)}) %reduce-scatter.7.cloned.1.call-update) | async-done | bytes 301072
  179.8 1.7 reshape.21
  181.5 0.3 copy.18
  181.8 54.2 %all-reduce.2 = (f32[3,448,112]{2,1,0:T(8,128)}, f32[3,448,112]{2,1,0:T(8,128)}) all-reduce(bf16[3,448,112]{2,1,0:T(8,128)(2,1)S(1)} %copy.18, bf16[3,448,112]{2,1,0:T(8,128)(2,1)S(1)} %copy.20), channel_id=1, replica_groups=mesh['groups'=2,'seq'=4,'dp'=4] {'seq'}, use_global_device_ids=true, to_apply=%region_1.0 | all-reduce | flops 301056 | bytes 1806336 | tf_op jit(solution)/shard_map/psum | solution.py:81
  (34 shorter events, 0.1 us)
Async XLA Ops:
  7.2 4.5 %copy-start.2 = (bf16[1,1024,448]{1,2,0:T(8,128)(2,1)S(1)}, bf16[1,1024,448]{1,2,0:T(8,128)(2,1)}, u32[]{:S(2)}) copy-start(bf16[1,1024,448]{1,2,0:T(8,128)(2,1)} %param.4) | copy-start | bytes 2752516
  7.2 26.8 %all-gather.3.cloned.1.call-start = ((), (), s32[]{:S(2)}) async-start(), calls=%async_computation.2 | async-start | bytes 2293760 | tf_op jit(solution)/shard_map/all_gather | solution.py:37
  9.4 47.9 %all-gather.5.cloned.1.call-start = ((), (), s32[]{:S(2)}) async-start(), calls=%async_computation.3 | async-start | bytes 2293760 | tf_op jit(solution)/shard_map/all_gather | solution.py:55
  11.6 150.4 %reduce-scatter.9.cloned.1.call-start = ((), (), s32[]{:S(2)}) async-start(), calls=%async_computation.5 | async-start | bytes 1576960
  13.2 65.6 %collective-permute-start = (bf16[1024,448]{0,1:T(8,128)(2,1)}, bf16[1024,448]{0,1:T(8,128)(2,1)}, u32[]{:S(2)}, u32[]{:S(2)}) collective-permute-start(bf16[1024,448]{0,1:T(8,128)(2,1)} %fusion.26), channel_id=1, source_target_pairs={{0,8},{4,12},{1,9},{5,13},{2,10},{6,14},{3,11},{7,15},{16,24},{20,... | collective-permute-start | bytes 2752520 | tf_op jit(solution)/shard_map/ppermute | solution.py:11
  20.1 60.7 %collective-permute-start.1 = (bf16[1024,448]{0,1:T(8,128)(2,1)}, bf16[1024,448]{0,1:T(8,128)(2,1)}, u32[]{:S(2)}, u32[]{:S(2)}) collective-permute-start(bf16[1024,448]{0,1:T(8,128)(2,1)} %fusion.26), channel_id=1, source_target_pairs={{8,0},{12,4},{9,1},{13,5},{10,2},{14,6},{11,3},{15,7},{24,16},{28,... | collective-permute-start | bytes 2752520 | tf_op jit(solution)/shard_map/ppermute | solution.py:11
  21.4 63.8 %collective-permute-start.2 = (bf16[1024,448]{0,1:T(8,128)(2,1)}, bf16[1024,448]{0,1:T(8,128)(2,1)}, u32[]{:S(2)}, u32[]{:S(2)}) collective-permute-start(bf16[1024,448]{0,1:T(8,128)(2,1)} %bitcast), channel_id=1, source_target_pairs={} | collective-permute-start | bytes 2752520 | tf_op jit(solution)/shard_map/ppermute | solution.py:11
  66.0 12.8 %copy-start = (bf16[1,448,448]{2,1,0:T(8,128)(2,1)}, bf16[1,448,448]{2,1,0:T(8,128)(2,1)S(1)}, u32[]{:S(2)}) copy-start(bf16[1,448,448]{2,1,0:T(8,128)(2,1)S(1)} %copy.21) | copy-start | bytes 1204228
  68.0 5.4 %copy-start.6 = (bf16[1,448,448]{1,0,2:T(2,128)(2,1)S(1)}, bf16[1,448,448]{1,0,2:T(2,128)(2,1)}, u32[]{:S(2)}) copy-start(bf16[1,448,448]{1,0,2:T(2,128)(2,1)} %get-tuple-element.6) | copy-start | bytes 1204228
  69.9 4.8 %copy-start.8 = (bf16[1,448,448]{2,1,0:T(8,128)(2,1)S(1)}, bf16[1,448,448]{2,1,0:T(8,128)(2,1)}, u32[]{:S(2)}) copy-start(bf16[1,448,448]{2,1,0:T(8,128)(2,1)} %copy.22) | copy-start | bytes 1204228
  78.8 1.9 copy-start.11
  82.8 2.4 copy-start.17
  89.2 2.8 %copy-start.10 = (bf16[1,448,448]{2,1,0:T(8,128)(2,1)S(1)}, bf16[1,448,448]{2,1,0:T(8,128)(2,1)}, u32[]{:S(2)}) copy-start(bf16[1,448,448]{2,1,0:T(8,128)(2,1)} %copy.24) | copy-start | bytes 1204228
  91.7 3.4 %copy-start.5 = (bf16[1,448,448]{1,0,2:T(2,128)(2,1)S(1)}, bf16[1,448,448]{1,0,2:T(2,128)(2,1)}, u32[]{:S(2)}) copy-start(bf16[1,448,448]{1,0,2:T(2,128)(2,1)} %get-tuple-element.5) | copy-start | bytes 1204228
  91.7 4.8 %copy-start.7 = (f32[1024,448]{0,1:T(8,128)S(1)}, f32[1024,448]{0,1:T(8,128)}, u32[]{:S(2)}) copy-start(f32[1024,448]{0,1:T(8,128)} %fusion.57) | copy-start | bytes 5505028
  91.8 88.0 %reduce-scatter.7.cloned.1.call-start = ((), (), s32[]{:S(2)}) async-start(), calls=%async_computation.4 | async-start | bytes 1576960
  96.5 10.0 %copy-start.3 = (bf16[1,1024,448]{1,2,0:T(8,128)(2,1)S(1)}, bf16[1,1024,448]{1,2,0:T(8,128)(2,1)}, u32[]{:S(2)}) copy-start(bf16[1,1024,448]{1,2,0:T(8,128)(2,1)} %param.4) | copy-start | bytes 2752516
  100.7 6.7 %copy-start.13 = (bf16[1024,448]{0,1:T(8,128)(2,1)}, bf16[1024,448]{0,1:T(8,128)(2,1)S(1)}, u32[]{:S(2)}) copy-start(bf16[1024,448]{0,1:T(8,128)(2,1)S(1)} %fusion.17) | copy-start | bytes 2752516
  100.7 24.5 %collective-permute-start.4 = (bf16[1024,448]{0,1:T(8,128)(2,1)S(1)}, bf16[1024,448]{0,1:T(8,128)(2,1)S(1)}, u32[]{:S(2)}, u32[]{:S(2)}) collective-permute-start(bf16[1024,448]{0,1:T(8,128)(2,1)S(1)} %fusion.17), channel_id=1, source_target_pairs={{0,8},{4,12},{1,9},{5,13},{2,10},{6,14},{3,11},{7,15},{16,24},{20,... | collective-permute-start | bytes 2752520 | tf_op jit(solution)/shard_map/ppermute | solution.py:11
  105.2 44.7 %collective-permute-start.3 = (bf16[1024,448]{0,1:T(8,128)(2,1)S(1)}, bf16[1024,448]{0,1:T(8,128)(2,1)S(1)}, u32[]{:S(2)}, u32[]{:S(2)}) collective-permute-start(bf16[1024,448]{0,1:T(8,128)(2,1)S(1)} %fusion.17), channel_id=1, source_target_pairs={{8,0},{12,4},{9,1},{13,5},{10,2},{14,6},{11,3},{15,7},{24,16},{28,... | collective-permute-start | bytes 2752520 | tf_op jit(solution)/shard_map/ppermute | solution.py:11
  125.2 0.9 copy-start.18
  149.9 0.9 copy-start.15
  153.6 2.5 %copy-start.9 = (bf16[1,448,448]{2,1,0:T(8,128)(2,1)S(1)}, bf16[1,448,448]{2,1,0:T(8,128)(2,1)}, u32[]{:S(2)}) copy-start(bf16[1,448,448]{2,1,0:T(8,128)(2,1)} %copy.22) | copy-start | bytes 1204228
  153.6 2.5 %copy-start.14 = (bf16[1024,448]{0,1:T(8,128)(2,1)S(1)}, bf16[1024,448]{0,1:T(8,128)(2,1)}, u32[]{:S(2)}) copy-start(bf16[1024,448]{0,1:T(8,128)(2,1)} %copy-done.13) | copy-start | bytes 2752516
  156.2 1.0 copy-start.1
  156.2 1.3 copy-start.16
  157.5 1.2 copy-start.4
  157.5 1.3 copy-start.12
  157.5 1.8 copy-start.19
Sparse Core Ops, SparseCore 0:
  10.1 23.8 all-gather.2
  36.1 21.1 all-gather.4
  91.9 26.2 reduce-scatter.8
  156.3 23.4 reduce-scatter.6
where the time goes:
time: 243 us
  waiting for transfers between devices  85.6 us (35%)
  blocking collectives  54.2 us (22%)
  local copies, waits for them, and re-layouts  44.6 us (18%)
  matrix products  26.1 us (11%)
  starting transfers between devices  15.9 us (7%)
  between operations  14.1 us (6%)
    psum x1, blocking collectives, on_device(): lax.psum(lax.psum_scatter(part_one, 'dp', scatter_dimension=2, tiled=True...  54.2 us
    ppermute x5, waiting for transfers between devices, shifted(): return lax.ppermute(block, axis, route)  41.6 us
    unnamed x56, local copies, waits for them, and re-layouts  32.2 us
    all_gather x1, waiting for transfers between devices, on_device(): full_two = lax.all_gather(weight_two, 'dp', axis=2, tiled=True)  17.2 us
    unnamed x6, waiting for transfers between devices  15.8 us
    ppermute x5, starting transfers between devices, shifted(): return lax.ppermute(block, axis, route)  15.6 us
    dot_general x6, matrix products, back_product(): lax.dot_general(tap, weight, (((1,), (1,)), ((), ())), preferred_element_...  14.4 us
    all_gather x1, waiting for transfers between devices, on_device(): full_one = lax.all_gather(first_weight_matrix, 'dp', axis=2, tiled=True)  11 us
  transfers between devices with their start and end apart: 9, of which 5 were waited for; matrix products, arithmetic and copies ran while one was open for 24% of the time, Pallas kernels for 0%

commit v1 on v0

--- a/solution.py
+++ b/solution.py
@@ -78,8 +78,12 @@
     part_one = jnp.stack(
         [outer_terms(input_activation, first_layer_taps[k], factor) for k in range(3)]
     ).astype(jnp.bfloat16)
-    grad_one = lax.psum(
-        lax.psum_scatter(part_one, "dp", scatter_dimension=2, tiled=True).astype(jnp.float32), "seq"
+    grad_one = jnp.sum(
+        lax.all_gather(
+            lax.psum_scatter(part_one, "dp", scatter_dimension=2, tiled=True).astype(jnp.float32),
+            "seq",
+        ),
+        axis=0,
     )
     return (input_grad.reshape(inputs.shape), grad_one, grad_two)
 

time: 243 us -> 283 us (1.16)
  waiting for transfers between devices: 85.6 us -> 127 us
  other arithmetic: 1.96 us -> 5.76 us
    all_gather x0 -> x1, waiting for transfers between devices: none -> 21.8 us  [on_device(): lax.all_gather(lax.psum_scatter(part_one, 'dp', scatter_dimension=2, tile...]
    unnamed x6 -> x7, waiting for transfers between devices: 15.8 us -> 35.4 us
    dot_general x6, matrix products: 14.4 us -> 11.4 us  [back_product(): lax.dot_general(tap, weight, (((1,), (1,)), ((), ())), preferred_element_...]
    reduce_sum x0 -> x1, other arithmetic: none -> 2.9 us  [on_device(): jnp.sum(lax.all_gather(lax.psum_scatter(part_one, 'dp', scatter_dimension...]
  transfers between devices with their start and end apart: 9 -> 10, of which waited for: 5 -> 7; matrix products, arithmetic and copies ran while one was open for 24% -> 19% of each run, Pallas kernels for 0% -> 0%
where the time goes in v1:
time: 283 us
  waiting for transfers between devices  127 us (45%)
  blocking collectives  51.4 us (18%)
  local copies, waits for them, and re-layouts  44.5 us (16%)
  matrix products  24.2 us (9%)
  starting transfers between devices  15.8 us (6%)
  between operations  14.1 us (5%)
  other arithmetic  5.76 us (2%)
    psum x1, blocking collectives, on_device(): lax.psum(lax.psum_scatter(part_two, 'dp', scatter_dimension=2, tiled=True...  51.4 us
    ppermute x5, waiting for transfers between devices, shifted(): return lax.ppermute(block, axis, route)  41.4 us
    unnamed x7, waiting for transfers between devices  35.4 us
    unnamed x56, local copies, waits for them, and re-layouts  32.1 us
    all_gather x1, waiting for transfers between devices, on_device(): lax.all_gather(lax.psum_scatter(part_one, 'dp', scatter_dimension=2, tile...  21.8 us
    all_gather x1, waiting for transfers between devices, on_device(): full_two = lax.all_gather(weight_two, 'dp', axis=2, tiled=True)  17.2 us
    ppermute x5, starting transfers between devices, shifted(): return lax.ppermute(block, axis, route)  15.6 us
    dot_general x6, matrix products, back_product(): lax.dot_general(tap, weight, (((1,), (1,)), ((), ())), preferred_element_...  11.4 us
  transfers between devices with their start and end apart: 10, of which 7 were waited for; matrix products, arithmetic and copies ran while one was open for 19% of the time, Pallas kernels for 0%

profile of v1, /device:TPU:0, one launch (start us, length us, event | category | flops | bytes accessed | tf_op | source)
XLA Modules:
  0.0 282.5 jit_solution(13720083953673352323)
XLA Ops:
  7.2 0.0 all-gather.5.cloned.1.call-start
  7.2 2.2 copy.9
  9.4 0.0 all-gather.5.cloned.1.call-update
  9.4 0.0 all-gather.7.cloned.1.call-start
  9.5 2.1 copy.13
  11.6 0.0 all-gather.7.cloned.1.call-update
  11.6 0.0 reduce-scatter.7.cloned.1.call-start
  11.7 1.6 fusion.26
  13.2 6.9 %collective-permute-start = (bf16[1024,448]{0,1:T(8,128)(2,1)}, bf16[1024,448]{0,1:T(8,128)(2,1)}, u32[]{:S(2)}, u32[]{:S(2)}) collective-permute-start(bf16[1024,448]{0,1:T(8,128)(2,1)} %fusion.26), channel_id=1, source_target_pairs={{0,8},{4,12},{1,9},{5,13},{2,10},{6,14},{3,11},{7,15},{16,24},{20,... | collective-permute-start | bytes 2752520 | tf_op jit(solution)/shard_map/ppermute | solution.py:11
  20.1 1.3 collective-permute-start.1
  21.4 1.6 collective-permute-start.2
  23.0 11.0 %all-gather.5.cloned.1.call-done = bf16[3,448,448]{1,0,2:T(4,128)(2,1)} async-done(((bf16[3,448,112]{1,0,2:T(4,128)(2,1)}), bf16[3,448,448]{1,0,2:T(4,128)(2,1)}) %all-gather.5.cloned.1.call-update) | async-done | bytes 1204240 | tf_op jit(solution)/shard_map/all_gather | solution.py:37
  34.0 6.1 %fusion.88 = (bf16[1,448,448]{1,0,2:T(2,128)(2,1)S(1)}, bf16[1,448,448]{1,0,2:T(2,128)(2,1)}, bf16[1,448,448]{1,0,2:T(2,128)(2,1)S(1)}) fusion(bf16[3,448,448]{1,0,2:T(4,128)(2,1)} %all-gather.5.cloned.1.call-done), kind=kLoop, calls=%fused_computation.93 | loop fusion | bytes 2408448 | tf_op jit(solution)/shard_map/slice | solution.py:51
  40.1 17.2 %all-gather.7.cloned.1.call-done = bf16[3,448,448]{1,0,2:T(4,128)(2,1)} async-done(((bf16[3,448,112]{1,0,2:T(4,128)(2,1)}), bf16[3,448,448]{1,0,2:T(4,128)(2,1)}) %all-gather.7.cloned.1.call-update) | async-done | bytes 1204240 | tf_op jit(solution)/shard_map/all_gather | solution.py:55
  57.3 6.3 %fusion.87 = (bf16[1,448,448]{1,0,2:T(2,128)(2,1)}, bf16[1,448,448]{1,0,2:T(2,128)(2,1)}, bf16[1,448,448]{1,0,2:T(2,128)(2,1)}) fusion(bf16[3,448,448]{1,0,2:T(4,128)(2,1)} %all-gather.7.cloned.1.call-done), kind=kLoop, calls=%fused_computation.92 | loop fusion | bytes 2408448 | tf_op jit(solution)/shard_map/slice | solution.py:59
  63.6 2.4 copy.22
  66.0 2.2 fusion.46
  68.3 1.3 copy.21
  69.6 2.0 copy.23
  71.6 3.5 %copy.24 = bf16[1,448,448]{2,1,0:T(8,128)(2,1)} copy(bf16[1,448,448]{1,0,2:T(2,128)(2,1)} %get-tuple-element.5) | data formatting | bytes 802816
  75.1 2.0 copy.25
  77.1 1.3 copy.26
  78.4 2.0 fusion.57
  80.4 1.9 fusion.74
  82.4 2.0 fusion.59
  84.4 2.1 fusion.27
  86.4 3.5 %fusion.17 = bf16[1024,448]{0,1:T(8,128)(2,1)S(1)} fusion(bf16[1024,448]{0,1:T(8,128)(2,1)S(1)} %fusion.27, f32[1024,448]{0,1:T(8,128)S(1)} %fusion.59, f32[1024,448]{0,1:T(8,128)S(1)} %fusion.57, bf16[1024,448]{0,1:T(8,128)(2,1)} %collective-permute-done.2, bf16[1,448,448]{2,1,0:T(8,128)(2,1)S(1)} %copy.26, bf16[1,1024,448]{1,2,0:T(8,128)(2,1)} %param.5), kind=kOutput, calls=%fused_computation.27 | convolution fusion | flops 422051840 | bytes 7741440 | tf_op jit(solution)/shard_map/dot_general | solution.py:26
  90.0 4.4 %collective-permute-start.4 = (bf16[1024,448]{0,1:T(8,128)(2,1)S(1)}, bf16[1024,448]{0,1:T(8,128)(2,1)S(1)}, u32[]{:S(2)}, u32[]{:S(2)}) collective-permute-start(bf16[1024,448]{0,1:T(8,128)(2,1)S(1)} %fusion.17), channel_id=1, source_target_pairs={{0,8},{4,12},{1,9},{5,13},{2,10},{6,14},{3,11},{7,15},{16,24},{20,... | collective-permute-start | bytes 2752520 | tf_op jit(solution)/shard_map/ppermute | solution.py:11
  94.4 1.5 collective-permute-start.3
  95.9 0.8 fusion.43
  96.7 17.7 %collective-permute-done.4 = bf16[1024,448]{0,1:T(8,128)(2,1)S(1)} collective-permute-done((bf16[1024,448]{0,1:T(8,128)(2,1)S(1)}, bf16[1024,448]{0,1:T(8,128)(2,1)S(1)}, u32[]{:S(2)}, u32[]{:S(2)}) %collective-permute-start.4) | collective-permute-done | bytes 917536 | tf_op jit(solution)/shard_map/ppermute | solution.py:11
  114.4 0.8 fusion.42
  115.2 0.1 copy-done.18
  115.3 23.7 %collective-permute-done.3 = bf16[1024,448]{0,1:T(8,128)(2,1)S(1)} collective-permute-done((bf16[1024,448]{0,1:T(8,128)(2,1)S(1)}, bf16[1024,448]{0,1:T(8,128)(2,1)S(1)}, u32[]{:S(2)}, u32[]{:S(2)}) %collective-permute-start.3) | collective-permute-done | bytes 917536 | tf_op jit(solution)/shard_map/ppermute | solution.py:11
  139.0 0.9 copy-done.14
  140.0 0.8 fusion.44
  140.8 0.2 pad_maximum_fusion
  141.0 1.8 copy.17
  142.8 2.5 reshape.22
  145.3 0.0 reduce-scatter.9.cloned.1.call-start
  145.4 2.0 fusion.40
  147.4 2.0 fusion.41
  149.4 0.2 pad_maximum_fusion.1
  149.6 1.8 copy.19
  151.4 2.5 reshape.24
  154.0 0.0 all-gather.9.cloned.1.call-start
  154.0 14.9 %reduce-scatter.7.cloned.1.call-done = bf16[112,1344]{1,0:T(8,128)(2,1)} async-done(((bf16[448,1344]{1,0:T(8,128)(2,1)}), bf16[112,1344]{1,0:T(8,128)(2,1)}) %reduce-scatter.7.cloned.1.call-update) | async-done | bytes 301072
  168.9 1.7 reshape.23
  170.7 0.3 copy.18
  171.0 0.9 all_gather.20
  171.9 0.6 fusion.69
  172.6 0.3 copy-done.1
  172.9 0.3 copy-done.15
  173.2 0.6 fusion.72
  173.9 0.5 copy-done.3
  174.4 0.1 copy-done.11
  174.5 0.3 copy-done.19
  174.8 2.7 fusion.52
  177.5 20.4 %reduce-scatter.9.cloned.1.call-done = bf16[112,1344]{1,0:T(8,128)(2,1)} async-done(((bf16[448,1344]{1,0:T(8,128)(2,1)}), bf16[112,1344]{1,0:T(8,128)(2,1)}) %reduce-scatter.9.cloned.1.call-update) | async-done | bytes 301072
  197.8 1.7 reshape.25
  199.6 0.3 copy.20
  199.9 51.4 %all-reduce.1 = f32[3,448,112]{2,1,0:T(8,128)} all-reduce(bf16[3,448,112]{2,1,0:T(8,128)(2,1)S(1)} %copy.20), channel_id=1, replica_groups=mesh['groups'=2,'seq'=4,'dp'=4] {'seq'}, use_global_device_ids=true, to_apply=%region_3.0 | all-reduce | flops 150528 | bytes 903168 | tf_op jit(solution)/shard_map/psum | solution.py:66
  251.3 21.8 %all-gather.9.cloned.1.call-done = f32[12,448,112]{2,1,0:T(8,128)} async-done(((f32[3,448,112]{2,1,0:T(8,128)}), f32[12,448,112]{2,1,0:T(8,128)}) %all-gather.9.cloned.1.call-update) | async-done | bytes 2408464 | tf_op jit(solution)/shard_map/all_gather | solution.py:82
  273.1 2.9 %reduce_sum.9 = f32[3,448,112]{2,1,0:T(8,128)} reduce(f32[4,3,448,112]{3,2,1,0:T(8,128)} %bitcast.122, f32[]{:T(128)} %constant.16.clone.1), dimensions={0}, to_apply=%region_1.0 | reduce | flops 451584 | bytes 3010564 | tf_op jit(solution)/shard_map/reduce_sum | solution.py:81
  (39 shorter events, 0.1 us)
Async XLA Ops:
  7.2 4.5 %copy-start.2 = (bf16[1,1024,448]{1,2,0:T(8,128)(2,1)S(1)}, bf16[1,1024,448]{1,2,0:T(8,128)(2,1)}, u32[]{:S(2)}) copy-start(bf16[1,1024,448]{1,2,0:T(8,128)(2,1)} %param.4) | copy-start | bytes 2752516
  7.2 26.8 %all-gather.5.cloned.1.call-start = ((), (), s32[]{:S(2)}) async-start(), calls=%async_computation.2 | async-start | bytes 2293760 | tf_op jit(solution)/shard_map/all_gather | solution.py:37
  9.4 47.9 %all-gather.7.cloned.1.call-start = ((), (), s32[]{:S(2)}) async-start(), calls=%async_computation.3 | async-start | bytes 2293760 | tf_op jit(solution)/shard_map/all_gather | solution.py:55
  11.6 157.3 %reduce-scatter.7.cloned.1.call-start = ((), (), s32[]{:S(2)}) async-start(), calls=%async_computation.5 | async-start | bytes 1576960
  13.2 67.2 %collective-permute-start = (bf16[1024,448]{0,1:T(8,128)(2,1)}, bf16[1024,448]{0,1:T(8,128)(2,1)}, u32[]{:S(2)}, u32[]{:S(2)}) collective-permute-start(bf16[1024,448]{0,1:T(8,128)(2,1)} %fusion.26), channel_id=1, source_target_pairs={{0,8},{4,12},{1,9},{5,13},{2,10},{6,14},{3,11},{7,15},{16,24},{20,... | collective-permute-start | bytes 2752520 | tf_op jit(solution)/shard_map/ppermute | solution.py:11
  20.1 64.2 %collective-permute-start.1 = (bf16[1024,448]{0,1:T(8,128)(2,1)}, bf16[1024,448]{0,1:T(8,128)(2,1)}, u32[]{:S(2)}, u32[]{:S(2)}) collective-permute-start(bf16[1024,448]{0,1:T(8,128)(2,1)} %fusion.26), channel_id=1, source_target_pairs={{8,0},{12,4},{9,1},{13,5},{10,2},{14,6},{11,3},{15,7},{24,16},{28,... | collective-permute-start | bytes 2752520 | tf_op jit(solution)/shard_map/ppermute | solution.py:11
  21.4 61.0 %collective-permute-start.2 = (bf16[1024,448]{0,1:T(8,128)(2,1)}, bf16[1024,448]{0,1:T(8,128)(2,1)}, u32[]{:S(2)}, u32[]{:S(2)}) collective-permute-start(bf16[1024,448]{0,1:T(8,128)(2,1)} %bitcast), channel_id=1, source_target_pairs={} | collective-permute-start | bytes 2752520 | tf_op jit(solution)/shard_map/ppermute | solution.py:11
  66.0 2.3 copy-start.6
  69.6 10.8 %copy-start = (bf16[1,448,448]{2,1,0:T(8,128)(2,1)}, bf16[1,448,448]{2,1,0:T(8,128)(2,1)S(1)}, u32[]{:S(2)}) copy-start(bf16[1,448,448]{2,1,0:T(8,128)(2,1)S(1)} %copy.21) | copy-start | bytes 1204228
  69.6 7.5 %copy-start.4 = (bf16[1,448,448]{1,0,2:T(2,128)(2,1)S(1)}, bf16[1,448,448]{1,0,2:T(2,128)(2,1)}, u32[]{:S(2)}) copy-start(bf16[1,448,448]{1,0,2:T(2,128)(2,1)} %get-tuple-element.3) | copy-start | bytes 1204228
  71.6 3.5 %copy-start.5 = (bf16[1,448,448]{1,0,2:T(2,128)(2,1)S(1)}, bf16[1,448,448]{1,0,2:T(2,128)(2,1)}, u32[]{:S(2)}) copy-start(bf16[1,448,448]{1,0,2:T(2,128)(2,1)} %get-tuple-element.4) | copy-start | bytes 1204228
  80.4 2.0 copy-start.8
  82.3 2.0 copy-start.9
  82.3 2.0 copy-start.10
  86.4 3.6 %copy-start.16 = (bf16[1024,448]{0,1:T(8,128)(2,1)}, bf16[1024,448]{0,1:T(8,128)(2,1)S(1)}, u32[]{:S(2)}) copy-start(bf16[1024,448]{0,1:T(8,128)(2,1)S(1)} %fusion.27) | copy-start | bytes 2752516
  90.0 6.7 %copy-start.12 = (bf16[1024,448]{0,1:T(8,128)(2,1)}, bf16[1024,448]{0,1:T(8,128)(2,1)S(1)}, u32[]{:S(2)}) copy-start(bf16[1024,448]{0,1:T(8,128)(2,1)S(1)} %fusion.17) | copy-start | bytes 2752516
  90.0 24.3 %collective-permute-start.4 = (bf16[1024,448]{0,1:T(8,128)(2,1)S(1)}, bf16[1024,448]{0,1:T(8,128)(2,1)S(1)}, u32[]{:S(2)}, u32[]{:S(2)}) collective-permute-start(bf16[1024,448]{0,1:T(8,128)(2,1)S(1)} %fusion.17), channel_id=1, source_target_pairs={{0,8},{4,12},{1,9},{5,13},{2,10},{6,14},{3,11},{7,15},{16,24},{20,... | collective-permute-start | bytes 2752520 | tf_op jit(solution)/shard_map/ppermute | solution.py:11
  94.4 44.7 %collective-permute-start.3 = (bf16[1024,448]{0,1:T(8,128)(2,1)S(1)}, bf16[1024,448]{0,1:T(8,128)(2,1)S(1)}, u32[]{:S(2)}, u32[]{:S(2)}) collective-permute-start(bf16[1024,448]{0,1:T(8,128)(2,1)S(1)} %fusion.17), channel_id=1, source_target_pairs={{8,0},{12,4},{9,1},{13,5},{10,2},{14,6},{11,3},{15,7},{24,16},{28,... | collective-permute-start | bytes 2752520 | tf_op jit(solution)/shard_map/ppermute | solution.py:11
  114.4 1.0 copy-start.18
  139.0 0.9 copy-start.14
  142.8 2.6 copy-start.17
  145.3 52.5 %reduce-scatter.9.cloned.1.call-start = ((), (), s32[]{:S(2)}) async-start(), calls=%async_computation.6 | async-start | bytes 1576960
  153.9 18.0 %copy-start.7 = (bf16[1,448,448]{2,1,0:T(8,128)(2,1)S(1)}, bf16[1,448,448]{2,1,0:T(8,128)(2,1)}, u32[]{:S(2)}) copy-start(bf16[1,448,448]{2,1,0:T(8,128)(2,1)} %copy-done.6) | copy-start | bytes 1204228
  153.9 18.0 %copy-start.13 = (bf16[1024,448]{0,1:T(8,128)(2,1)S(1)}, bf16[1024,448]{0,1:T(8,128)(2,1)}, u32[]{:S(2)}) copy-start(bf16[1024,448]{0,1:T(8,128)(2,1)} %copy-done.12) | copy-start | bytes 2752516
  154.0 119.1 %all-gather.9.cloned.1.call-start = ((), (), s32[]{:S(2)}) async-start(), calls=%async_computation.4 | async-start | bytes 3440640 | tf_op jit(solution)/shard_map/all_gather | solution.py:82
  171.9 1.0 copy-start.1
  171.9 1.3 copy-start.15
  173.2 1.2 copy-start.3
  173.2 1.3 copy-start.11
  173.2 1.6 copy-start.19
Sparse Core Ops, SparseCore 0:
  10.1 23.8 all-gather.4
  36.1 21.1 all-gather.6
  145.4 23.4 reduce-scatter.6
  171.6 26.2 reduce-scatter.8
  199.8 73.2 all-gather.8
